TPU v7x, 32 devices: a whole 2x2x4 slice. The times are simulated.
32 devices in a mesh: ctx: 16 (over z, y, x), fsdp: 2 (over core).
Axes of the slice: x: 2, y: 2, z: 4, core: 2. Of those that a mesh axis runs over, the one named last changes fastest.
Arguments:
- xbc: bfloat16 [4096, 9216], P(('fsdp', 'ctx')), may hold values from -6 to 6
- dt: bfloat16 [4096, 128], P(('fsdp', 'ctx')), may hold values from -5 to 5
- conv_weight: float32 [4, 9216], P(None, 'fsdp'), may hold values from -3 to 3
- conv_bias: float32 [9216], P('fsdp'), may hold values from -0.5 to 0.5
- dt_bias: float32 [128], P('fsdp'), may hold values from -1 to 1
- a_log: float32 [128], P('fsdp'), may hold values from -14 to -3
- skip: float32 [128], P('fsdp'), may hold values from 0.5 to 2
- norm_gain: float32 [8192], P('fsdp'), may hold values from 0.5 to 1.5
Outputs:
- mixed: bfloat16 [4096, 8192], P(('fsdp', 'ctx'))
All inputs are finite; a program needn't handle non-finite values.
Results may differ from a plain program's by a relative error of at most 0.0051.
Values may be sent and summed in bfloat16 or wider, within the bound.
A program may use at most 128 MiB of HBM per device.

v0:
```python
import jax
import jax.numpy as jnp
from jax import lax
from jax.experimental import pallas as pl
from jax.experimental.pallas import tpu as pltpu
from jax.sharding import PartitionSpec as P

P_SIZE = 64
N = 128
GROUPS = 4
HALO = 16
WIDTH = 256
F32, BF16 = jnp.float32, jnp.bfloat16
ANY = pl.BlockSpec(memory_space=pl.ANY)


def place():
    f, c = lax.axis_index("fsdp"), lax.axis_index("ctx")
    nz = lax.axis_size("ctx") // GROUPS
    nf = lax.axis_size("fsdp")
    g, z = lax.rem(c, GROUPS), c // GROUPS
    return f, c, g, z, nz, nf, f * nz + z


def device(seg, g, nz):
    return {"fsdp": seg // nz, "ctx": lax.rem(seg, nz) * GROUPS + g}


def lanes(index, size):
    return pl.ds(pl.multiple_of(index * size, 128), size)


def hi_lo(v):
    hi = v.astype(BF16)
    return jnp.concatenate([hi, (v - hi.astype(F32)).astype(BF16)], axis=1)


def dot(a, b, dims=((1,), (0,))):
    return lax.dot_general(a, b, (dims, ((), ())), preferred_element_type=F32)


def fill_selection(sel, g):
    heads, width = sel.shape[0] // 2, sel.shape[1]
    per_group = width // P_SIZE
    row = lax.broadcasted_iota(jnp.int32, sel.shape, 0)
    col = lax.broadcasted_iota(jnp.int32, sel.shape, 1)
    row = jnp.where(row >= heads, row - heads, row)
    sel[...] = jnp.where(row == g * per_group + col // P_SIZE, 1.0, 0.0).astype(BF16)


def silu_conv(ext, start, cw, at, size):
    rows = ext.shape[0] - 8
    total = cw[4:5, at]
    for k in range(4):
        total = total + cw[k : k + 1, at] * ext[5 + k : 5 + k + rows, start : start + size]
    return (total / (1.0 + jnp.exp(-total))).astype(BF16)


def mixer_kernel(x, dt, cw_in, gn_in, out,
                 raw, raw_bc, dts, halo, cw, gn, sel, ext, keys, left, source, decay_2, carry_2,
                 vec_2, z_buf, p_buf, q_buf, r_buf, y_out, y_in, o_buf,
                 xsend, xrecv, bsend, brecv, psend, precv, hsend, hrecv, csend, crecv,
                 osend, orecv, xown, own_sem, out_sem):
    f, c, g, z, nz, nf, seg = place()
    last = nz * nf - 1
    rows = x.shape[0]
    chunks = raw.shape[0]
    gw = chunks * WIDTH
    di = gw * GROUPS
    heads = dt.shape[1]

    def peer(d):
        return {"fsdp": f, "ctx": z * GROUPS + lax.rem(g + d, GROUPS)}

    def sibling(d):
        return {"fsdp": lax.rem(f + d, nf), "ctx": c}

    barrier = pltpu.get_barrier_semaphore()
    for d in range(1, GROUPS):
        pl.semaphore_signal(barrier, inc=1, device_id=peer(d))
    for d in range(1, nf):
        pl.semaphore_signal(barrier, inc=1, device_id=sibling(d))

    @pl.when(seg > 0)
    def _():
        pl.semaphore_signal(barrier, inc=1, device_id=device(seg - 1, g, nz))

    @pl.when(jnp.logical_and(seg > 0, g < GROUPS - 1))
    def _():
        pl.semaphore_signal(barrier, inc=1, device_id=device(seg - 1, GROUPS - 1, nz))

    more = jnp.where(seg < last, jnp.where(g == GROUPS - 1, GROUPS, 1), 0)
    pl.semaphore_wait(barrier, GROUPS - 1 + nf - 1 + more)

    def b_at(p):
        return pl.ds(pl.multiple_of(di + p * N, 128), N)

    def c_at(p):
        return pl.ds(pl.multiple_of(di + (GROUPS + p) * N, 128), N)

    mine = pl.ds(pl.multiple_of(g * rows, 128), rows)

    def halo_copies():
        out = []
        tail = pl.ds(rows - HALO, HALO)
        for p in range(GROUPS):
            parts = [(x.at[tail, lanes(p, gw)], halo.at[:, 0:gw]),
                     (x.at[tail, b_at(p)], halo.at[:, gw : gw + N]),
                     (x.at[tail, c_at(p)], halo.at[:, gw + N : gw + 2 * N])]
            for k, (src, dst) in enumerate(parts):
                out.append(pltpu.make_async_remote_copy(
                    src, dst, hsend.at[p, k], hrecv.at[k], device_id=device(seg + 1, p, nz)))
        return out

    sends_halo = jnp.logical_and(g == GROUPS - 1, seg < last)

    @pl.when(sends_halo)
    def _():
        for copy in halo_copies():
            copy.start()

    params = [(cw_in, cw.at[:, lanes(f, cw_in.shape[1])]), (gn_in, gn.at[:, lanes(f, gn_in.shape[1])])]

    def small(p):
        return [(x.at[:, b_at(p)], raw_bc.at[mine, 0:N]),
                (x.at[:, c_at(p)], raw_bc.at[mine, N : 2 * N]), (dt, dts.at[g])]

    first = []
    for d in range(1, nf):
        for k, (src, dst) in enumerate(params):
            first.append(pltpu.make_async_remote_copy(
                src, dst, psend.at[d, k], precv.at[d, k], device_id=sibling(d)))
    for d in (2, 1, 3):
        for k, (src, dst) in enumerate(small(lax.rem(g + d, GROUPS))):
            first.append(pltpu.make_async_remote_copy(
                src, dst, bsend.at[d, k], brecv.at[d, k], device_id=peer(d)))
    for k, (src, dst) in enumerate(small(g) + params):
        first.append(pltpu.make_async_copy(src, dst, own_sem.at[k]))
    for copy in first:
        copy.start()

    def pieces(q):
        out = []
        for d in (2, 1, 3):
            p = lax.rem(g + d, GROUPS)
            out.append(pltpu.make_async_remote_copy(
                x.at[:, lanes(p * chunks + q, WIDTH)], raw.at[q, mine], xsend.at[d, q],
                xrecv.at[d, q], device_id=peer(d)))
        out.append(pltpu.make_async_copy(
            x.at[:, lanes(g * chunks + q, WIDTH)], raw.at[q, mine], xown.at[q]))
        return out

    @pl.loop(0, chunks)
    def _(q):
        for copy in pieces(q):
            copy.start()

    @pl.when(seg == 0)
    def _():
        q_buf[...] = jnp.zeros_like(q_buf)

    fill_selection(sel, g)
    for copy in first:
        copy.wait()

    @pl.when(seg > 0)
    def _():
        for copy in halo_copies()[:3]:
            copy.wait_recv()

    def before(at, size):
        return jnp.where(seg > 0, halo[HALO - 8 :, at].astype(F32), 0.0)

    ext[0:8, :] = before(pl.ds(gw, 2 * N), 2 * N)
    ext[8:, :] = raw_bc[...].astype(F32)
    keys[...] = silu_conv(ext, 0, cw, b_at(g), N)
    queries = silu_conv(ext, N, cw, c_at(g), N)
    vectors = cw[5:8, 0:heads]
    for d in range(1, nf):
        vectors = vectors + cw[5:8, pl.ds(d * cw_in.shape[1], heads)]
    lower = (lax.broadcasted_iota(jnp.int32, (rows, rows), 0)
             >= lax.broadcasted_iota(jnp.int32, (rows, rows), 1))
    ones = jnp.where(lower, 1.0, 0.0)
    scale = jnp.exp(vectors[1:2, :])
    decayed = jnp.ones((1, heads), F32)
    for j in range(GROUPS):
        at = pl.ds(j * rows, rows)
        delta = dts[j].astype(F32) + vectors[0:1, :]
        delta = jnp.maximum(delta, 0.0) + jnp.log1p(jnp.exp(-jnp.abs(delta)))
        cum = lax.dot_general(ones, -scale * delta, (((1,), (0,)), ((), ())),
                              precision=lax.Precision.HIGHEST, preferred_element_type=F32)
        decay = jnp.exp(cum)
        source[j] = hi_lo(delta * jnp.exp(-cum))
        decay_2[j] = hi_lo(decay)
        carry_2[j] = hi_lo(decay * decayed)
        block_decay = decay[rows - 1 : rows, :]
        decayed = decayed * block_decay
        vec_2[j] = hi_lo(jnp.concatenate(
            [vectors[2:3, :], block_decay, decayed, jnp.zeros((5, heads), F32)], axis=0))
        mine_q = queries[j * rows : (j + 1) * rows]
        scores = jnp.where(lower, dot(mine_q, keys[at, :], ((1,), (1,))), 0.0).astype(BF16)
        left[j] = jnp.concatenate([scores, mine_q], axis=1)

    def local_step(q):
        for copy in pieces(q)[:3]:
            copy.wait_recv()
        pieces(q)[3].wait()
        here = lanes(q, WIDTH)
        ext[0:8, :] = before(here, WIDTH)
        ext[8:, :] = raw[q].astype(F32)
        act = silu_conv(ext, 0, cw, lanes(g * chunks + q, WIDTH), WIDTH)
        pick = sel[:, here]
        state = jnp.zeros((N, WIDTH), F32)
        for j in range(GROUPS):
            values = act[j * rows : (j + 1) * rows].astype(F32)
            weighted = (values * dot(source[j], pick)).astype(BF16)
            vec = dot(vec_2[j], pick)
            inner = dot(left[j], jnp.concatenate([weighted, state.astype(BF16)], axis=0))
            z_buf[q, j] = dot(decay_2[j], pick) * inner + vec[0:1, :] * values
            state = vec[1:2, :] * (state + dot(keys[pl.ds(j * rows, rows), :], weighted, ((0,), (0,))))
        p_buf[q] = state

    def hop(q):
        return pltpu.make_async_remote_copy(
            r_buf.at[q], q_buf.at[q], csend.at[q], crecv.at[q], device_id=device(seg + 1, g, nz))

    def back(d, q):
        return pltpu.make_async_remote_copy(
            y_out.at[lax.rem(g + d, GROUPS), q], y_in.at[g, q], osend.at[d, q], orecv.at[d, q],
            device_id=peer(d))

    def carry_step(q):
        pick = sel[:, lanes(q, WIDTH)]

        @pl.when(seg > 0)
        def _():
            hop(q).wait_recv()

        state = q_buf[q]

        @pl.when(seg < last)
        def _():
            through = dot(vec_2[GROUPS - 1], pick)[2:3, :]
            r_buf[q] = (p_buf[q] + through * state.astype(F32)).astype(r_buf.dtype)
            hop(q).start()

        low = state.astype(BF16)
        for j in range(GROUPS):
            carried = dot(left[j, :, N:], low) * dot(carry_2[j], pick)
            y_out[j, q] = (z_buf[q, j] + carried).astype(BF16)
        for d in range(1, GROUPS):
            back(d, q).start()
        y_in[g, q] = y_out[g, q]

    lag = seg if nz * nf <= chunks else jnp.where(seg < chunks, seg, chunks)

    @pl.loop(0, 2 * chunks)
    def _(i):
        @pl.when(i < chunks)
        def _():
            local_step(i)

        @pl.when(jnp.logical_and(i >= lag, i < lag + chunks))
        def _():
            carry_step(i - lag)

    @pl.loop(0, chunks)
    def _(q):
        for copy in pieces(q)[:3]:
            copy.wait_send()
        for d in range(1, GROUPS):
            back(d, q).wait()

    def finished(p):
        at = lanes(p, gw)
        return pltpu.make_async_copy(o_buf.at[:, at], out.at[:, at], out_sem.at[p])

    @pl.loop(0, GROUPS)
    def _(p):
        total = jnp.zeros((rows, WIDTH), F32)
        for q in range(chunks):
            y = y_in[p, q].astype(F32)
            total = total + y * y
        norm = lax.rsqrt(jnp.sum(total, axis=1, keepdims=True) * (1.0 / gw) + 1e-05)
        for q in range(chunks):
            at = lanes(p * chunks + q, WIDTH)
            o_buf[:, at] = (y_in[p, q].astype(F32) * norm * gn[0:1, at]).astype(BF16)
        finished(p).start()

    @pl.when(seg < last)
    def _():
        @pl.loop(0, chunks)
        def _(q):
            hop(q).wait_send()

    @pl.when(sends_halo)
    def _():
        for copy in halo_copies():
            copy.wait_send()

    for p in range(GROUPS):
        finished(p).wait()


def mixer(x, dt, cw, gn):
    rows, ch = x.shape
    heads = dt.shape[1]
    nf = lax.axis_size("fsdp")
    segments = nf * (lax.axis_size("ctx") // GROUPS)
    gw = heads * P_SIZE // GROUPS
    chunks = gw // WIDTH
    length = rows * GROUPS
    link = BF16 if segments <= 8 else F32
    vm, dma = pltpu.VMEM, pltpu.SemaphoreType.DMA
    return pl.pallas_call(
        mixer_kernel,
        out_shape=jax.ShapeDtypeStruct((rows, gw * GROUPS), BF16),
        in_specs=[ANY] * 4,
        out_specs=ANY,
        scratch_shapes=[
            vm((chunks, length, WIDTH), BF16),
            vm((length, 2 * N), BF16),
            vm((GROUPS, rows, heads), BF16),
            vm((HALO, gw + 2 * N), BF16),
            vm((8, ch), F32),
            vm((1, gw * GROUPS), F32),
            vm((2 * heads, gw), BF16),
            vm((8 + length, WIDTH), F32),
            vm((length, N), BF16),
            vm((GROUPS, rows, 2 * N), BF16),
            vm((GROUPS, rows, 2 * heads), BF16),
            vm((GROUPS, rows, 2 * heads), BF16),
            vm((GROUPS, rows, 2 * heads), BF16),
            vm((GROUPS, 8, 2 * heads), BF16),
            vm((chunks, GROUPS, rows, WIDTH), F32),
            vm((chunks, N, WIDTH), F32),
            vm((chunks, N, WIDTH), link),
            vm((chunks, N, WIDTH), link),
            vm((GROUPS, chunks, rows, WIDTH), BF16),
            vm((GROUPS, chunks, rows, WIDTH), BF16),
            vm((rows, gw * GROUPS), BF16),
            dma((GROUPS, chunks)), dma((GROUPS, chunks)), dma((GROUPS, 3)), dma((GROUPS, 3)),
            dma((nf, 2)), dma((nf, 2)), dma((GROUPS, 3)), dma((3,)),
            dma((chunks,)), dma((chunks,)), dma((GROUPS, chunks)), dma((GROUPS, chunks)),
            dma((chunks,)), dma((5,)), dma((GROUPS,)),
        ],
        compiler_params=pltpu.CompilerParams(
            collective_id=0, has_side_effects=True, vmem_limit_bytes=48 << 20),
        name="mixer",
    )(x, dt, cw, gn)


def local(xbc, dt, conv_weight, conv_bias, dt_bias, a_log, skip, norm_gain):
    heads = dt.shape[1]
    own = dt_bias.shape[0]
    width = conv_bias.shape[0]
    small = lax.dynamic_update_slice(
        jnp.zeros((3, width), F32), jnp.stack([dt_bias, a_log, skip]),
        (0, lax.axis_index("fsdp") * own))
    params = jnp.concatenate([conv_weight, conv_bias[None], small], axis=0)
    return mixer(xbc, dt, params, norm_gain[None])


def solution(mesh):
    placed = (
        P(("fsdp", "ctx"), None),
        P(("fsdp", "ctx"), None),
        P(None, "fsdp"),
        P("fsdp"),
        P("fsdp"),
        P("fsdp"),
        P("fsdp"),
        P("fsdp"),
    )
    return jax.shard_map(
        local, mesh=mesh, in_specs=placed, out_specs=P(("fsdp", "ctx"), None), check_vma=False
    )
```

profile of v0, /device:TPU:27, one launch (start us, length us, event | category | flops | bytes accessed | tf_op | source)
XLA Modules:
  0.0 69.6 jit_solution(18151927365167902846)
XLA Ops:
  0.0 0.7 %pad_maximum_fusion.1 = f32[3,64]{1,0:T(4,128)S(1)} fusion(f32[1,64]{1,0:T(1,128)} %bitcast.5, f32[1,64]{1,0:T(1,128)} %bitcast.6, f32[1,64]{1,0:T(1,128)} %bitcast.7), kind=kLoop, calls=%fused_computation.1 | loop fusion | flops 384 | bytes 1536 | tf_op jit(solution)/shard_map/stack | solution.py:358
  0.7 0.7 %broadcast_in_dim.9 = f32[1,4608]{1,0:T(1,128)S(1)} reshape(f32[4608]{0:T(1024)} %param.11) | data formatting | bytes 36864 | tf_op jit(solution)/shard_map/broadcast_in_dim | solution.py:360
  1.5 0.3 dynamic_update_slice.3
  1.7 0.9 %pad_maximum_fusion.cw_in = f32[8,4608]{1,0:T(8,128)S(1)} fusion(f32[3,4608]{1,0:T(4,128)S(1)} %dynamic_update_slice.3, f32[1,4608]{1,0:T(1,128)S(1)} %broadcast_in_dim.9, f32[4,4608]{1,0:T(4,128)} %param.10), kind=kLoop, calls=%fused_computation | loop fusion | flops 73728 | bytes 294912 | tf_op jit(solution)/shard_map/concatenate | solution.py:360
  2.7 0.0 copy-start
  2.7 1.7 %copy-done = bf16[128,9216]{1,0:T(8,128)(2,1)S(1)} copy-done((bf16[128,9216]{1,0:T(8,128)(2,1)S(1)}, bf16[128,9216]{1,0:T(8,128)(2,1)}, u32[]{:S(2)}) %copy-start) | copy-done | bytes 2359320
  4.3 0.0 copy-start.1
  4.3 0.8 %copy-done.1 = bf16[128,128]{1,0:T(8,128)(2,1)S(1)} copy-done((bf16[128,128]{1,0:T(8,128)(2,1)S(1)}, bf16[128,128]{1,0:T(8,128)(2,1)}, u32[]{:S(2)}) %copy-start.1) | copy-done | bytes 32792
  5.1 0.0 copy-start.2
  5.1 0.7 %copy-done.2 = f32[4096]{0:T(1024)S(1)} copy-done((f32[4096]{0:T(1024)S(1)}, f32[4096]{0:T(1024)}, u32[]{:S(2)}) %copy-start.2) | copy-done | bytes 16408
  5.8 62.4 %mixer.1 = bf16[128,8192]{1,0:T(8,128)(2,1)S(1)} custom-call(bf16[128,9216]{1,0:T(8,128)(2,1)S(1)} %copy-done, bf16[128,128]{1,0:T(8,128)(2,1)S(1)} %copy-done.1, f32[8,4608]{1,0:T(8,128)S(1)} %pad_maximum_fusion.cw_in, f32[1,4096]{1,0:T(1,128)S(1)} %bitcast.4), custom_call_target="tpu_custom_call" | custom-call | tf_op jit(solution)/shard_map/mixer/pallas_call | solution.py:315
  68.3 1.3 %copy.11 = bf16[128,8192]{1,0:T(8,128)(2,1)} copy(bf16[128,8192]{1,0:T(8,128)(2,1)S(1)} %mixer.1) | data formatting | bytes 4194304
  (1 shorter events, 0.0 us)
Async XLA Ops:
  2.7 1.7 %copy-start = (bf16[128,9216]{1,0:T(8,128)(2,1)S(1)}, bf16[128,9216]{1,0:T(8,128)(2,1)}, u32[]{:S(2)}) copy-start(bf16[128,9216]{1,0:T(8,128)(2,1)} %x.1) | copy-start | bytes 7077892
  4.3 0.8 %copy-start.1 = (bf16[128,128]{1,0:T(8,128)(2,1)S(1)}, bf16[128,128]{1,0:T(8,128)(2,1)}, u32[]{:S(2)}) copy-start(bf16[128,128]{1,0:T(8,128)(2,1)} %dt.1) | copy-start | bytes 98308
  5.1 0.7 %copy-start.2 = (f32[4096]{0:T(1024)S(1)}, f32[4096]{0:T(1024)}, u32[]{:S(2)}) copy-start(f32[4096]{0:T(1024)} %param.15) | copy-start | bytes 49156
where the time goes:
time: 70 us; the launch traced here: 69.6 us
  Pallas kernels  62.4 us (89%)
  local copies, waits for them, and re-layouts  5.47 us (8%)
  other arithmetic  1.64 us (2%)
    pallas_call x1, Pallas kernels, mixer(): pl.pallas_call(mixer_kernel, out_shape=jax.ShapeDtypeStruct((rows, gw * G...  62.4 us
    unnamed x7, local copies, waits for them, and re-layouts  4.46 us

commit v1 on v0

--- a/solution.py
+++ b/solution.py
@@ -58,7 +58,7 @@
 
 def mixer_kernel(x, dt, cw_in, gn_in, out,
                  raw, raw_bc, dts, halo, cw, gn, sel, ext, keys, left, source, decay_2, carry_2,
-                 vec_2, z_buf, p_buf, q_buf, r_buf, y_out, y_in, o_buf,
+                 vec_2, z_buf, p_buf, q_buf, r_buf, y_out, y_in, o_buf, squares,
                  xsend, xrecv, bsend, brecv, psend, precv, hsend, hrecv, csend, crecv,
                  osend, orecv, xown, own_sem, out_sem):
     f, c, g, z, nz, nf, seg = place()
@@ -160,6 +160,7 @@
         q_buf[...] = jnp.zeros_like(q_buf)
 
     fill_selection(sel, g)
+    squares[...] = jnp.zeros_like(squares)
     for copy in first:
         copy.wait()
 
@@ -175,9 +176,10 @@
     ext[8:, :] = raw_bc[...].astype(F32)
     keys[...] = silu_conv(ext, 0, cw, b_at(g), N)
     queries = silu_conv(ext, N, cw, c_at(g), N)
+    owner = lax.broadcasted_iota(jnp.int32, (3, heads), 1) // (heads // nf)
     vectors = cw[5:8, 0:heads]
     for d in range(1, nf):
-        vectors = vectors + cw[5:8, pl.ds(d * cw_in.shape[1], heads)]
+        vectors = jnp.where(owner == d, cw[5:8, pl.ds(d * cw_in.shape[1], heads)], vectors)
     lower = (lax.broadcasted_iota(jnp.int32, (rows, rows), 0)
              >= lax.broadcasted_iota(jnp.int32, (rows, rows), 1))
     ones = jnp.where(lower, 1.0, 0.0)
@@ -266,10 +268,11 @@
 
     @pl.loop(0, chunks)
     def _(q):
-        for copy in pieces(q)[:3]:
-            copy.wait_send()
         for d in range(1, GROUPS):
-            back(d, q).wait()
+            back(d, q).wait_recv()
+        for p in range(GROUPS):
+            y = y_in[p, q].astype(F32)
+            squares[p] = squares[p] + y * y
 
     def finished(p):
         at = lanes(p, gw)
@@ -277,15 +280,18 @@
 
     @pl.loop(0, GROUPS)
     def _(p):
-        total = jnp.zeros((rows, WIDTH), F32)
-        for q in range(chunks):
-            y = y_in[p, q].astype(F32)
-            total = total + y * y
-        norm = lax.rsqrt(jnp.sum(total, axis=1, keepdims=True) * (1.0 / gw) + 1e-05)
+        norm = lax.rsqrt(jnp.sum(squares[p], axis=1, keepdims=True) * (1.0 / gw) + 1e-05)
         for q in range(chunks):
             at = lanes(p * chunks + q, WIDTH)
             o_buf[:, at] = (y_in[p, q].astype(F32) * norm * gn[0:1, at]).astype(BF16)
         finished(p).start()
+
+    @pl.loop(0, chunks)
+    def _(q):
+        for copy in pieces(q)[:3]:
+            copy.wait_send()
+        for d in range(1, GROUPS):
+            back(d, q).wait_send()
 
     @pl.when(seg < last)
     def _():
@@ -339,25 +345,28 @@
             vm((GROUPS, chunks, rows, WIDTH), BF16),
             vm((GROUPS, chunks, rows, WIDTH), BF16),
             vm((rows, gw * GROUPS), BF16),
+            vm((GROUPS, rows, WIDTH), F32),
             dma((GROUPS, chunks)), dma((GROUPS, chunks)), dma((GROUPS, 3)), dma((GROUPS, 3)),
             dma((nf, 2)), dma((nf, 2)), dma((GROUPS, 3)), dma((3,)),
             dma((chunks,)), dma((chunks,)), dma((GROUPS, chunks)), dma((GROUPS, chunks)),
             dma((chunks,)), dma((5,)), dma((GROUPS,)),
         ],
         compiler_params=pltpu.CompilerParams(
-            collective_id=0, has_side_effects=True, vmem_limit_bytes=48 << 20),
+            collective_id=0, has_side_effects=True, vmem_limit_bytes=62 << 20),
         name="mixer",
     )(x, dt, cw, gn)
 
 
 def local(xbc, dt, conv_weight, conv_bias, dt_bias, a_log, skip, norm_gain):
-    heads = dt.shape[1]
-    own = dt_bias.shape[0]
-    width = conv_bias.shape[0]
-    small = lax.dynamic_update_slice(
-        jnp.zeros((3, width), F32), jnp.stack([dt_bias, a_log, skip]),
-        (0, lax.axis_index("fsdp") * own))
-    params = jnp.concatenate([conv_weight, conv_bias[None], small], axis=0)
+    width, own = conv_bias.shape[0], dt_bias.shape[0]
+    shape = (8, width)
+    row = lax.broadcasted_iota(jnp.int32, shape, 0)
+    params = lax.pad(conv_weight, 0.0, ((0, 4, 0), (0, 0, 0)))
+    params = jnp.where(row == 4, jnp.broadcast_to(conv_bias, shape), params)
+    for k, vector in enumerate((dt_bias, a_log, skip)):
+        repeated = sum(lax.pad(vector, 0.0, ((at, width - own - at, 0),))
+                       for at in range(0, dt.shape[1], own))
+        params = jnp.where(row == 5 + k, jnp.broadcast_to(repeated, shape), params)
     return mixer(xbc, dt, params, norm_gain[None])
 
 

time: 70 us -> 70 us (level)
  local copies, waits for them, and re-layouts: 5.47 us -> 3.1 us
  other arithmetic: 1.64 us -> 3.28 us
  Pallas kernels: 62.4 us -> 63.4 us
    select_n x0 -> x1, other arithmetic: none -> 1.65 us  [local(): params = jnp.where(row == 5 + k, jnp.broadcast_to(repeated, shape), params)]
    add x0 -> x2, other arithmetic: none -> 1.62 us  [local(): sum((lax.pad(vector, 0.0, ((at, width - own - at, 0),)) for at in range(0...]
    unnamed x7 -> x1, local copies, waits for them, and re-layouts: 4.46 us -> 3.1 us
    pallas_call x1, Pallas kernels: 62.4 us -> 63.4 us  [mixer(): pl.pallas_call(mixer_kernel, out_shape=jax.ShapeDtypeStruct((rows, gw * G...]
    concatenate x1 -> x0, other arithmetic: 0.94 us -> none  [local(): params = jnp.concatenate([conv_weight, conv_bias[None], small], axis=0)]
    broadcast_in_dim x2 -> x0, local copies, waits for them, and re-layouts: 0.75 us -> none  [the longest x1 0.74 us: local(): params = jnp.concatenate([conv_weight, conv_bias[None], small], axis=0)]
where the time goes in v1:
time: 70 us; the launch traced here: 69.8 us
  Pallas kernels  63.4 us (91%)
  other arithmetic  3.28 us (5%)
  local copies, waits for them, and re-layouts  3.1 us (4%)
    pallas_call x1, Pallas kernels, mixer(): pl.pallas_call(mixer_kernel, out_shape=jax.ShapeDtypeStruct((rows, gw * G...  63.4 us
    unnamed x1, local copies, waits for them, and re-layouts  3.1 us
    select_n x1, other arithmetic, local(): params = jnp.where(row == 5 + k, jnp.broadcast_to(repeated, shape), params)  1.65 us
    add x2, other arithmetic, local(): sum((lax.pad(vector, 0.0, ((at, width - own - at, 0),)) for at in range(0...  1.62 us

profile of v1, /device:TPU:27, one launch (start us, length us, event | category | flops | bytes accessed | tf_op | source)
XLA Modules:
  0.0 69.8 jit_solution(7956450592819671097)
XLA Ops:
  0.0 0.8 %pad_add_fusion.2 = f32[4608]{0:T(1024)S(1)} fusion(f32[64]{0:T(128)} %param.14), kind=kLoop, calls=%fused_computation.3 | loop fusion | flops 4608 | bytes 18688 | tf_op jit(solution)/shard_map/add | solution.py:367
  0.8 0.8 %pad_add_fusion = (f32[4608]{0:T(1024)S(1)}, f32[4608]{0:T(1024)S(1)}) fusion(f32[64]{0:T(128)} %param.12, f32[64]{0:T(128)} %param.13), kind=kLoop, calls=%fused_computation.1 | loop fusion | flops 9216 | bytes 37376 | tf_op jit(solution)/shard_map/add | solution.py:367
  1.6 1.7 %select_select_fusion.cw_in = f32[8,4608]{1,0:T(8,128)} fusion(f32[4,4608]{1,0:T(4,128)} %param.10, f32[4608]{0:T(1024)} %param.11, f32[4608]{0:T(1024)S(1)} %get-tuple-element.5, f32[4608]{0:T(1024)S(1)} %get-tuple-element.6, f32[4608]{0:T(1024)S(1)} %pad_add_fusion.2, pred[8]{0:T(512)(128)(4,1)S(1)} %get-tuple-element.7, ...), kind=kLoop, calls=%fused_computation | loop fusion | flops 147456 | bytes 294944 | tf_op jit(solution)/shard_map/jit(_where)/select_n | solution.py:369
  3.3 63.4 %mixer.1 = bf16[128,8192]{1,0:T(8,128)(2,1)} custom-call(bf16[128,9216]{1,0:T(8,128)(2,1)} %x.15, bf16[128,128]{1,0:T(8,128)(2,1)} %dt.1, f32[8,4608]{1,0:T(8,128)} %select_select_fusion.cw_in, f32[1,4096]{1,0:T(1,128)} %bitcast.1), custom_call_target="tpu_custom_call" | custom-call | tf_op jit(solution)/shard_map/mixer/pallas_call | solution.py:321
  66.7 3.1 %copy.10 = bf16[128,8192]{1,0:T(8,128)(2,1)} copy(bf16[128,8192]{1,0:T(8,128)(2,1)} %mixer.1) | data formatting | bytes 4194304
  (2 shorter events, 0.0 us)

commit v2 on v1

--- a/solution.py
+++ b/solution.py
@@ -176,10 +176,9 @@
     ext[8:, :] = raw_bc[...].astype(F32)
     keys[...] = silu_conv(ext, 0, cw, b_at(g), N)
     queries = silu_conv(ext, N, cw, c_at(g), N)
-    owner = lax.broadcasted_iota(jnp.int32, (3, heads), 1) // (heads // nf)
     vectors = cw[5:8, 0:heads]
     for d in range(1, nf):
-        vectors = jnp.where(owner == d, cw[5:8, pl.ds(d * cw_in.shape[1], heads)], vectors)
+        vectors = vectors + cw[5:8, pl.ds(d * cw_in.shape[1], heads)]
     lower = (lax.broadcasted_iota(jnp.int32, (rows, rows), 0)
              >= lax.broadcasted_iota(jnp.int32, (rows, rows), 1))
     ones = jnp.where(lower, 1.0, 0.0)
@@ -352,21 +351,19 @@
             dma((chunks,)), dma((5,)), dma((GROUPS,)),
         ],
         compiler_params=pltpu.CompilerParams(
-            collective_id=0, has_side_effects=True, vmem_limit_bytes=62 << 20),
+            collective_id=0, has_side_effects=True, vmem_limit_bytes=51 << 20),
         name="mixer",
     )(x, dt, cw, gn)
 
 
 def local(xbc, dt, conv_weight, conv_bias, dt_bias, a_log, skip, norm_gain):
-    width, own = conv_bias.shape[0], dt_bias.shape[0]
-    shape = (8, width)
-    row = lax.broadcasted_iota(jnp.int32, shape, 0)
-    params = lax.pad(conv_weight, 0.0, ((0, 4, 0), (0, 0, 0)))
-    params = jnp.where(row == 4, jnp.broadcast_to(conv_bias, shape), params)
-    for k, vector in enumerate((dt_bias, a_log, skip)):
-        repeated = sum(lax.pad(vector, 0.0, ((at, width - own - at, 0),))
-                       for at in range(0, dt.shape[1], own))
-        params = jnp.where(row == 5 + k, jnp.broadcast_to(repeated, shape), params)
+    heads = dt.shape[1]
+    own = dt_bias.shape[0]
+    width = conv_bias.shape[0]
+    small = lax.dynamic_update_slice(
+        jnp.zeros((3, width), F32), jnp.stack([dt_bias, a_log, skip]),
+        (0, lax.axis_index("fsdp") * own))
+    params = jnp.concatenate([conv_weight, conv_bias[None], small], axis=0)
     return mixer(xbc, dt, params, norm_gain[None])
 
 

time: 70 us -> 68.6 us (0.980)
  other arithmetic: 3.28 us -> 1.64 us
  local copies, waits for them, and re-layouts: 3.1 us -> 3.81 us
    select_n x1 -> x0, other arithmetic: 1.65 us -> none  [local(): params = jnp.where(row == 5 + k, jnp.broadcast_to(repeated, shape), params)]
    add x2 -> x0, other arithmetic: 1.62 us -> none  [local(): sum((lax.pad(vector, 0.0, ((at, width - own - at, 0),)) for at in range(0...]
    concatenate x0 -> x1, other arithmetic: none -> 0.94 us  [local(): params = jnp.concatenate([conv_weight, conv_bias[None], small], axis=0)]
    broadcast_in_dim x0 -> x2, local copies, waits for them, and re-layouts: none -> 0.75 us  [the longest x1 0.74 us: local(): params = jnp.concatenate([conv_weight, conv_bias[None], small], axis=0)]
    unnamed x1 -> x5, local copies, waits for them, and re-layouts: 3.1 us -> 2.79 us
where the time goes in v2:
time: 68.6 us; the launch traced here: 68.2 us
  Pallas kernels  62.8 us (92%)
  local copies, waits for them, and re-layouts  3.81 us (6%)
  other arithmetic  1.64 us (2%)
    pallas_call x1, Pallas kernels, mixer(): pl.pallas_call(mixer_kernel, out_shape=jax.ShapeDtypeStruct((rows, gw * G...  62.8 us
    unnamed x5, local copies, waits for them, and re-layouts  2.79 us

profile of v2, /device:TPU:27, one launch (start us, length us, event | category | flops | bytes accessed | tf_op | source)
XLA Modules:
  0.0 68.2 jit_solution(6979576550376426456)
XLA Ops:
  0.0 0.7 %pad_maximum_fusion.1 = f32[3,64]{1,0:T(4,128)S(1)} fusion(f32[1,64]{1,0:T(1,128)} %bitcast.5, f32[1,64]{1,0:T(1,128)} %bitcast.6, f32[1,64]{1,0:T(1,128)} %bitcast.7), kind=kLoop, calls=%fused_computation.1 | loop fusion | flops 384 | bytes 1536 | tf_op jit(solution)/shard_map/stack | solution.py:364
  0.7 0.7 %broadcast_in_dim.9 = f32[1,4608]{1,0:T(1,128)S(1)} reshape(f32[4608]{0:T(1024)} %param.11) | data formatting | bytes 36864 | tf_op jit(solution)/shard_map/broadcast_in_dim | solution.py:366
  1.5 0.3 dynamic_update_slice.3
  1.7 0.9 %pad_maximum_fusion.cw_in = f32[8,4608]{1,0:T(8,128)S(1)} fusion(f32[3,4608]{1,0:T(4,128)S(1)} %dynamic_update_slice.3, f32[1,4608]{1,0:T(1,128)S(1)} %broadcast_in_dim.9, f32[4,4608]{1,0:T(4,128)} %param.10), kind=kLoop, calls=%fused_computation | loop fusion | flops 73728 | bytes 294912 | tf_op jit(solution)/shard_map/concatenate | solution.py:366
  2.7 0.0 copy-start
  2.7 0.7 %copy-done = bf16[128,128]{1,0:T(8,128)(2,1)S(1)} copy-done((bf16[128,128]{1,0:T(8,128)(2,1)S(1)}, bf16[128,128]{1,0:T(8,128)(2,1)}, u32[]{:S(2)}) %copy-start) | copy-done | bytes 32792
  3.4 0.0 copy-start.1
  3.4 0.7 %copy-done.1 = f32[4096]{0:T(1024)S(1)} copy-done((f32[4096]{0:T(1024)S(1)}, f32[4096]{0:T(1024)}, u32[]{:S(2)}) %copy-start.1) | copy-done | bytes 16408
  4.2 62.8 %mixer.1 = bf16[128,8192]{1,0:T(8,128)(2,1)S(1)} custom-call(bf16[128,9216]{1,0:T(8,128)(2,1)} %x.1, bf16[128,128]{1,0:T(8,128)(2,1)S(1)} %copy-done, f32[8,4608]{1,0:T(8,128)S(1)} %pad_maximum_fusion.cw_in, f32[1,4096]{1,0:T(1,128)S(1)} %bitcast.4), custom_call_target="tpu_custom_call" | custom-call | tf_op jit(solution)/shard_map/mixer/pallas_call | solution.py:320
  66.9 1.3 %copy.11 = bf16[128,8192]{1,0:T(8,128)(2,1)} copy(bf16[128,8192]{1,0:T(8,128)(2,1)S(1)} %mixer.1) | data formatting | bytes 4194304
  (1 shorter events, 0.0 us)
Async XLA Ops:
  2.7 0.8 %copy-start = (bf16[128,128]{1,0:T(8,128)(2,1)S(1)}, bf16[128,128]{1,0:T(8,128)(2,1)}, u32[]{:S(2)}) copy-start(bf16[128,128]{1,0:T(8,128)(2,1)} %dt.1) | copy-start | bytes 98308
  3.4 0.7 %copy-start.1 = (f32[4096]{0:T(1024)S(1)}, f32[4096]{0:T(1024)}, u32[]{:S(2)}) copy-start(f32[4096]{0:T(1024)} %param.15) | copy-start | bytes 49156

commit v3 on v2

--- a/solution.py
+++ b/solution.py
@@ -56,8 +56,8 @@
     return (total / (1.0 + jnp.exp(-total))).astype(BF16)
 
 
-def mixer_kernel(x, dt, cw_in, gn_in, out,
-                 raw, raw_bc, dts, halo, cw, gn, sel, ext, keys, left, source, decay_2, carry_2,
+def mixer_kernel(x, dt, cw_in, out,
+                 raw, raw_bc, dts, halo, cw, sel, ext, keys, left, source, decay_2, carry_2,
                  vec_2, z_buf, p_buf, q_buf, r_buf, y_out, y_in, o_buf, squares,
                  xsend, xrecv, bsend, brecv, psend, precv, hsend, hrecv, csend, crecv,
                  osend, orecv, xown, own_sem, out_sem):
@@ -119,7 +119,7 @@
         for copy in halo_copies():
             copy.start()
 
-    params = [(cw_in, cw.at[:, lanes(f, cw_in.shape[1])]), (gn_in, gn.at[:, lanes(f, gn_in.shape[1])])]
+    params = [(cw_in, cw.at[:, lanes(f, cw_in.shape[1])])]
 
     def small(p):
         return [(x.at[:, b_at(p)], raw_bc.at[mine, 0:N]),
@@ -176,17 +176,18 @@
     ext[8:, :] = raw_bc[...].astype(F32)
     keys[...] = silu_conv(ext, 0, cw, b_at(g), N)
     queries = silu_conv(ext, N, cw, c_at(g), N)
-    vectors = cw[5:8, 0:heads]
+    vectors = cw[5:6, 0 : 3 * heads]
     for d in range(1, nf):
-        vectors = vectors + cw[5:8, pl.ds(d * cw_in.shape[1], heads)]
+        vectors = vectors + cw[5:6, pl.ds(d * cw_in.shape[1], 3 * heads)]
+    step_bias, rate_log, direct = (vectors[:, k * heads : (k + 1) * heads] for k in range(3))
     lower = (lax.broadcasted_iota(jnp.int32, (rows, rows), 0)
              >= lax.broadcasted_iota(jnp.int32, (rows, rows), 1))
     ones = jnp.where(lower, 1.0, 0.0)
-    scale = jnp.exp(vectors[1:2, :])
+    scale = jnp.exp(rate_log)
     decayed = jnp.ones((1, heads), F32)
     for j in range(GROUPS):
         at = pl.ds(j * rows, rows)
-        delta = dts[j].astype(F32) + vectors[0:1, :]
+        delta = dts[j].astype(F32) + step_bias
         delta = jnp.maximum(delta, 0.0) + jnp.log1p(jnp.exp(-jnp.abs(delta)))
         cum = lax.dot_general(ones, -scale * delta, (((1,), (0,)), ((), ())),
                               precision=lax.Precision.HIGHEST, preferred_element_type=F32)
@@ -197,7 +198,7 @@
         block_decay = decay[rows - 1 : rows, :]
         decayed = decayed * block_decay
         vec_2[j] = hi_lo(jnp.concatenate(
-            [vectors[2:3, :], block_decay, decayed, jnp.zeros((5, heads), F32)], axis=0))
+            [direct, block_decay, decayed, jnp.zeros((5, heads), F32)], axis=0))
         mine_q = queries[j * rows : (j + 1) * rows]
         scores = jnp.where(lower, dot(mine_q, keys[at, :], ((1,), (1,))), 0.0).astype(BF16)
         left[j] = jnp.concatenate([scores, mine_q], axis=1)
@@ -277,12 +278,18 @@
         at = lanes(p, gw)
         return pltpu.make_async_copy(o_buf.at[:, at], out.at[:, at], out_sem.at[p])
 
+    per = di // nf // WIDTH
+
+    def gain_of(i):
+        at = i // per * cw_in.shape[1] + lax.rem(i, per) * WIDTH
+        return cw[6:7, pl.ds(pl.multiple_of(at, 128), WIDTH)]
+
     @pl.loop(0, GROUPS)
     def _(p):
         norm = lax.rsqrt(jnp.sum(squares[p], axis=1, keepdims=True) * (1.0 / gw) + 1e-05)
         for q in range(chunks):
             at = lanes(p * chunks + q, WIDTH)
-            o_buf[:, at] = (y_in[p, q].astype(F32) * norm * gn[0:1, at]).astype(BF16)
+            o_buf[:, at] = (y_in[p, q].astype(F32) * norm * gain_of(p * chunks + q)).astype(BF16)
         finished(p).start()
 
     @pl.loop(0, chunks)
@@ -307,7 +314,7 @@
         finished(p).wait()
 
 
-def mixer(x, dt, cw, gn):
+def mixer(x, dt, cw):
     rows, ch = x.shape
     heads = dt.shape[1]
     nf = lax.axis_size("fsdp")
@@ -320,7 +327,7 @@
     return pl.pallas_call(
         mixer_kernel,
         out_shape=jax.ShapeDtypeStruct((rows, gw * GROUPS), BF16),
-        in_specs=[ANY] * 4,
+        in_specs=[ANY] * 3,
         out_specs=ANY,
         scratch_shapes=[
             vm((chunks, length, WIDTH), BF16),
@@ -328,7 +335,6 @@
             vm((GROUPS, rows, heads), BF16),
             vm((HALO, gw + 2 * N), BF16),
             vm((8, ch), F32),
-            vm((1, gw * GROUPS), F32),
             vm((2 * heads, gw), BF16),
             vm((8 + length, WIDTH), F32),
             vm((length, N), BF16),
@@ -346,14 +352,14 @@
             vm((rows, gw * GROUPS), BF16),
             vm((GROUPS, rows, WIDTH), F32),
             dma((GROUPS, chunks)), dma((GROUPS, chunks)), dma((GROUPS, 3)), dma((GROUPS, 3)),
-            dma((nf, 2)), dma((nf, 2)), dma((GROUPS, 3)), dma((3,)),
+            dma((nf, 1)), dma((nf, 1)), dma((GROUPS, 3)), dma((3,)),
             dma((chunks,)), dma((chunks,)), dma((GROUPS, chunks)), dma((GROUPS, chunks)),
-            dma((chunks,)), dma((5,)), dma((GROUPS,)),
+            dma((chunks,)), dma((4,)), dma((GROUPS,)),
         ],
         compiler_params=pltpu.CompilerParams(
             collective_id=0, has_side_effects=True, vmem_limit_bytes=51 << 20),
         name="mixer",
-    )(x, dt, cw, gn)
+    )(x, dt, cw)
 
 
 def local(xbc, dt, conv_weight, conv_bias, dt_bias, a_log, skip, norm_gain):
@@ -361,10 +367,14 @@
     own = dt_bias.shape[0]
     width = conv_bias.shape[0]
     small = lax.dynamic_update_slice(
-        jnp.zeros((3, width), F32), jnp.stack([dt_bias, a_log, skip]),
-        (0, lax.axis_index("fsdp") * own))
-    params = jnp.concatenate([conv_weight, conv_bias[None], small], axis=0)
-    return mixer(xbc, dt, params, norm_gain[None])
+        jnp.zeros((3, heads), F32), jnp.stack([dt_bias, a_log, skip]),
+        (0, lax.axis_index("fsdp") * own)).reshape(1, 3 * heads)
+    params = jnp.concatenate([
+        conv_weight, conv_bias[None],
+        jnp.pad(small, ((0, 0), (0, width - 3 * heads))),
+        jnp.pad(norm_gain[None], ((0, 1), (0, width - norm_gain.shape[0]))),
+    ], axis=0)
+    return mixer(xbc, dt, params)
 
 
 def solution(mesh):

time: 68.6 us -> 67.8 us (0.988)
  local copies, waits for them, and re-layouts: 3.81 us -> 3.07 us
    unnamed x5 -> x4, local copies, waits for them, and re-layouts: 2.79 us -> 2.08 us
where the time goes in v3:
time: 67.8 us; the launch traced here: 67.5 us
  Pallas kernels  62.7 us (92%)
  local copies, waits for them, and re-layouts  3.07 us (5%)
  other arithmetic  1.66 us (2%)
    pallas_call x1, Pallas kernels, mixer(): pl.pallas_call(mixer_kernel, out_shape=jax.ShapeDtypeStruct((rows, gw * G...  62.7 us
    unnamed x4, local copies, waits for them, and re-layouts  2.08 us

profile of v3, /device:TPU:27, one launch (start us, length us, event | category | flops | bytes accessed | tf_op | source)
XLA Modules:
  0.0 67.5 jit_solution(4896059946725566619)
XLA Ops:
  0.0 0.7 %pad_maximum_fusion = f32[3,64]{1,0:T(4,128)S(1)} fusion(f32[1,64]{1,0:T(1,128)} %bitcast.12, f32[1,64]{1,0:T(1,128)} %bitcast.13, f32[1,64]{1,0:T(1,128)} %bitcast.14), kind=kLoop, calls=%fused_computation.6 | loop fusion | flops 384 | bytes 1536 | tf_op jit(solution)/shard_map/stack | solution.py:370
  0.7 0.3 dynamic_update_slice.3
  1.0 0.7 %broadcast_in_dim.9 = f32[1,4608]{1,0:T(1,128)S(1)} reshape(f32[4608]{0:T(1024)} %param.11) | data formatting | bytes 36864 | tf_op jit(solution)/shard_map/broadcast_in_dim | solution.py:373
  1.7 1.0 %select_maximum_fusion.cw_in = f32[8,4608]{1,0:T(8,128)S(1)} fusion(f32[1,4096]{1,0:T(1,128)} %bitcast.9, f32[1,384]{1,0:T(1,128)S(1)} %bitcast.11, f32[1,4608]{1,0:T(1,128)S(1)} %broadcast_in_dim.9, f32[4,4608]{1,0:T(4,128)} %param.10), kind=kLoop, calls=%fused_computation.2 | loop fusion | flops 331776 | bytes 257536 | tf_op jit(solution)/shard_map/concatenate | solution.py:372
  2.7 0.0 copy-start
  2.7 0.7 %copy-done = bf16[128,128]{1,0:T(8,128)(2,1)S(1)} copy-done((bf16[128,128]{1,0:T(8,128)(2,1)S(1)}, bf16[128,128]{1,0:T(8,128)(2,1)}, u32[]{:S(2)}) %copy-start) | copy-done | bytes 32792
  3.4 62.7 %mixer.1 = bf16[128,8192]{1,0:T(8,128)(2,1)S(1)} custom-call(bf16[128,9216]{1,0:T(8,128)(2,1)} %x.5, bf16[128,128]{1,0:T(8,128)(2,1)S(1)} %copy-done, f32[8,4608]{1,0:T(8,128)S(1)} %select_maximum_fusion.cw_in), custom_call_target="tpu_custom_call" | custom-call | tf_op jit(solution)/shard_map/mixer/pallas_call | solution.py:327
  66.2 1.3 %copy.14 = bf16[128,8192]{1,0:T(8,128)(2,1)} copy(bf16[128,8192]{1,0:T(8,128)(2,1)S(1)} %mixer.1) | data formatting | bytes 4194304
  (2 shorter events, 0.0 us)
Async XLA Ops:
  2.7 0.8 %copy-start = (bf16[128,128]{1,0:T(8,128)(2,1)S(1)}, bf16[128,128]{1,0:T(8,128)(2,1)}, u32[]{:S(2)}) copy-start(bf16[128,128]{1,0:T(8,128)(2,1)} %dt.1) | copy-start | bytes 98308
